TPU v7x, 32 devices: a whole 2x2x4 slice. The times are simulated.
32 devices in a mesh: dp: 8 (over z, y), tp: 4 (over x, core).
Axes of the slice: x: 2, y: 2, z: 4, core: 2. Of those that a mesh axis runs over, the one named last changes fastest.
Arguments:
- tokens: bfloat16 [8, 2048, 768], P('dp', 'tp'), may hold values from -6 to 6
- cotangent: bfloat16 [8, 2048, 768], P('dp', 'tp'), may hold values from -6 to 6
- tags: int32 [8], P('dp'), may hold values from 0 to 7
- tag_weight: float32 [8], replicated, may hold values from 0.25 to 4
- query_weight: bfloat16 [768, 768], P(None, 'tp'), may hold values from -0.21875 to 0.21875
- key_value_weight: bfloat16 [768, 128], replicated, may hold values from -0.21875 to 0.21875
- output_weight: bfloat16 [768, 768], P('tp'), may hold values from -1.25 to 1.25
- up_weight: bfloat16 [768, 3072], P(None, 'tp'), may hold values from -0.21875 to 0.21875
- down_weight: bfloat16 [3072, 768], P('tp'), may hold values from -0.109375 to 0.109375
- norm_gain_one: float32 [768], replicated, may hold values from 0.25 to 1.75
- norm_bias_one: float32 [768], replicated, may hold values from -1.5 to 1.5
- norm_gain_two: float32 [768], replicated, may hold values from 0.25 to 1.75
- norm_bias_two: float32 [768], replicated, may hold values from -1.5 to 1.5
Outputs:
- block_out: bfloat16 [8, 2048, 768], P('dp', 'tp')
- grad_tokens: bfloat16 [8, 2048, 768], P('dp', 'tp')
- grad_query: float32 [768, 768], P(None, 'tp')
- grad_keyval: float32 [768, 128], replicated
- grad_output: float32 [768, 768], P('tp')
- grad_upward: float32 [768, 3072], P(None, 'tp')
- grad_downward: float32 [3072, 768], P('tp')
- grad_gain_one: float32 [768], replicated
- grad_bias_one: float32 [768], replicated
- grad_gain_two: float32 [768], replicated
- grad_bias_two: float32 [768], replicated
All inputs are finite; a program needn't handle non-finite values.
Results may differ from a plain program's by a relative error of at most 0.013.
Values may be sent and summed in bfloat16 or wider, within the bound.
A program may use at most 128 MiB of HBM per device.

v0:
```python
import jax
import jax.numpy as jnp
from jax import lax
from jax.sharding import PartitionSpec as P

HD = 64
ROT = 16


def layer_norm(values, gain_vec, shift_vec):
    row_mean = jnp.mean(values, axis=-1, keepdims=True)
    centred = values - row_mean
    variance = jnp.mean(centred * centred, axis=-1, keepdims=True)
    inverse = lax.rsqrt(variance + 1e-05)
    normal = centred * inverse
    return (normal * gain_vec + shift_vec, normal, inverse)


def norm_back(upstream, normal, inverse, gain_vec):
    scaled = upstream * gain_vec
    term_one = jnp.mean(scaled, axis=-1, keepdims=True)
    term_two = jnp.mean(scaled * normal, axis=-1, keepdims=True)
    return inverse * (scaled - term_one - normal * term_two)


def rot_angles(positions):
    frequencies = 10000.0 ** (-jnp.arange(0, ROT, 2, dtype=jnp.float32) / ROT)
    return positions.astype(jnp.float32)[:, None] * frequencies[None, :]


def rotate(values, angles, direction):
    half_rot = ROT // 2
    cosine = jnp.cos(angles)[:, None, :]
    sine_part = direction * jnp.sin(angles)[:, None, :]
    front_half = values[..., :half_rot]
    back_half = values[..., half_rot:ROT]
    return jnp.concatenate(
        [
            front_half * cosine - back_half * sine_part,
            back_half * cosine + front_half * sine_part,
            values[..., ROT:],
        ],
        axis=-1,
    )


def outer_sum(left, right):
    return lax.dot_general(
        left, right, (((0, 1), (0, 1)), ((), ())), preferred_element_type=jnp.float32
    )


def against(left, weight):
    return lax.dot_general(
        left, weight, (((2,), (1,)), ((), ())), preferred_element_type=jnp.float32
    )


def shards(
    tokens,
    cotangent,
    tags,
    tag_weight,
    query_weight,
    key_value_weight,
    output_weight,
    up_weight,
    down_weight,
    norm_gain_one,
    norm_bias_one,
    norm_gain_two,
    norm_bias_two,
):
    seq_dev, own_len, model_width = tokens.shape
    full_len = own_len * lax.axis_size("tp")
    heads_dev = query_weight.shape[1] // HD
    score_scale = HD ** (-0.5)
    block_rows = min(512, full_len)
    blocks = full_len // block_rows
    own_rows = tokens.astype(jnp.float32)
    full_angles = rot_angles(jnp.arange(full_len))
    first_normed, normal_one, inverse_one = layer_norm(own_rows, norm_gain_one, norm_bias_one)
    second_normed, normal_two, inverse_two = layer_norm(own_rows, norm_gain_two, norm_bias_two)
    low_one = first_normed.astype(jnp.bfloat16)
    low_two = second_normed.astype(jnp.bfloat16)
    rows_one, rows_two = (
        lax.all_gather(low_one, "tp", axis=1, tiled=True),
        lax.all_gather(low_two, "tp", axis=1, tiled=True),
    )
    key_value_rows = jnp.dot(rows_one, key_value_weight, preferred_element_type=jnp.float32)
    key_part = rotate(key_value_rows[:, :, None, :HD], full_angles, 1.0)[:, :, 0, :]
    key_value_rows = jnp.concatenate([key_part, key_value_rows[:, :, HD:]], axis=-1).astype(
        jnp.bfloat16
    )
    key_rows = key_value_rows[:, :, :HD]
    value_rows = key_value_rows[:, :, HD:]
    query_matrix = jnp.dot(rows_one, query_weight, preferred_element_type=jnp.float32).reshape(
        seq_dev, full_len, heads_dev, HD
    )
    query_matrix = rotate(query_matrix, full_angles, 1.0).astype(jnp.bfloat16)

    def block_scores(query_block, block_start):
        block_end = block_start + block_rows
        scores = (
            jnp.einsum(
                "sqhd,skd->sqhk",
                query_block,
                key_rows[:, :block_end],
                preferred_element_type=jnp.float32,
            )
            * score_scale
        )
        allowed = jnp.arange(block_end)[None, :] <= (block_start + jnp.arange(block_rows))[:, None]
        return jnp.where(allowed[None, :, None, :], scores, -1e30)

    context_list = []
    lse_list = []
    for block_index in range(blocks):
        block_start = block_index * block_rows
        block_end = block_start + block_rows
        scores = block_scores(query_matrix[:, block_start:block_end], block_start)
        row_top = jnp.max(scores, axis=-1, keepdims=True)
        weights = jnp.exp(scores - row_top)
        row_total = jnp.sum(weights, axis=-1, keepdims=True)
        weights_low = (weights / row_total).astype(jnp.bfloat16)
        context_list.append(
            jnp.einsum(
                "sqhk,skd->sqhd",
                weights_low,
                value_rows[:, :block_end],
                preferred_element_type=jnp.float32,
            )
        )
        lse_list.append(row_top + jnp.log(row_total))
    context_full = jnp.concatenate(context_list, axis=1)
    low_context = context_full.reshape(seq_dev, full_len, heads_dev * HD).astype(jnp.bfloat16)
    attention_branch = jnp.dot(low_context, output_weight, preferred_element_type=jnp.float32)
    hidden_rows = jnp.dot(rows_two, up_weight, preferred_element_type=jnp.float32)
    middle_rows = jax.nn.gelu(hidden_rows, approximate=False).astype(jnp.bfloat16)
    feedforward_branch = jnp.dot(middle_rows, down_weight, preferred_element_type=jnp.float32)
    branch = lax.psum_scatter(
        (attention_branch + feedforward_branch).astype(jnp.bfloat16),
        "tp",
        scatter_dimension=1,
        tiled=True,
    ).astype(jnp.float32)
    block_out = (own_rows + branch).astype(jnp.bfloat16)
    tag_ids = jnp.arange(tag_weight.shape[0], dtype=jnp.int32)
    row_weight = jnp.sum(
        jnp.where(tags[:, None] == tag_ids[None, :], tag_weight[None, :], 0.0), axis=1
    )
    upstream = cotangent.astype(jnp.float32) * row_weight[:, None, None]
    grad_rows = lax.all_gather(upstream.astype(jnp.bfloat16), "tp", axis=1, tiled=True)
    grad_output = outer_sum(low_context, grad_rows)
    grad_downward = outer_sum(middle_rows, grad_rows)
    grad_context = (
        against(grad_rows, output_weight)
        .astype(jnp.bfloat16)
        .reshape(seq_dev, full_len, heads_dev, HD)
    )
    grad_middle = against(grad_rows, down_weight)
    normal_cdf = 0.5 * (1.0 + lax.erf(hidden_rows * 0.7071067811865476))
    density = jnp.exp(-0.5 * hidden_rows * hidden_rows) * 0.3989422804014327
    grad_hidden = (grad_middle * (normal_cdf + hidden_rows * density)).astype(jnp.bfloat16)
    grad_upward = outer_sum(rows_two, grad_hidden)
    norm_part_two = against(grad_hidden, up_weight)
    grad_kv_full = jnp.zeros((seq_dev, full_len, 2 * HD), jnp.float32)
    query_grad_list = []
    for block_index in range(blocks):
        block_start = block_index * block_rows
        block_end = block_start + block_rows
        query_block = query_matrix[:, block_start:block_end]
        grad_block = grad_context[:, block_start:block_end]
        scores = block_scores(query_block, block_start)
        weights = jnp.exp(scores - lse_list[block_index])
        grad_weights = jnp.einsum(
            "sqhd,skd->sqhk",
            grad_block,
            value_rows[:, :block_end],
            preferred_element_type=jnp.float32,
        )
        row_delta = jnp.sum(
            grad_block.astype(jnp.float32) * context_list[block_index], axis=-1, keepdims=True
        )
        grad_scores = (weights * (grad_weights - row_delta)).astype(jnp.bfloat16)
        query_grad_list.append(
            jnp.einsum(
                "sqhk,skd->sqhd",
                grad_scores,
                key_rows[:, :block_end],
                preferred_element_type=jnp.float32,
            )
            * score_scale
        )
        grad_keys = (
            jnp.einsum(
                "sqhk,sqhd->skd", grad_scores, query_block, preferred_element_type=jnp.float32
            )
            * score_scale
        )
        grad_values = jnp.einsum(
            "sqhk,sqhd->skd",
            weights.astype(jnp.bfloat16),
            grad_block,
            preferred_element_type=jnp.float32,
        )
        grad_kv_full = grad_kv_full.at[:, :block_end].add(
            jnp.concatenate([grad_keys, grad_values], axis=-1)
        )
    grad_queries = jnp.concatenate(query_grad_list, axis=1)
    grad_queries = (
        rotate(grad_queries, full_angles, -1.0)
        .reshape(seq_dev, full_len, heads_dev * HD)
        .astype(jnp.bfloat16)
    )
    grad_query = outer_sum(rows_one, grad_queries)
    norm_part_one = against(grad_queries, query_weight)
    key_back = rotate(grad_kv_full[:, :, None, :HD], full_angles, -1.0)[:, :, 0, :]
    keyval_part = jnp.concatenate([key_back, grad_kv_full[:, :, HD:]], axis=-1)
    sum_one, sum_two, sum_keyval = (
        lax.psum_scatter(
            norm_part_one.astype(jnp.bfloat16), "tp", scatter_dimension=1, tiled=True
        ).astype(jnp.float32),
        lax.psum_scatter(
            norm_part_two.astype(jnp.bfloat16), "tp", scatter_dimension=1, tiled=True
        ).astype(jnp.float32),
        lax.psum_scatter(
            keyval_part.astype(jnp.bfloat16), "tp", scatter_dimension=1, tiled=True
        ).astype(jnp.float32),
    )
    low_keyval = sum_keyval.astype(jnp.bfloat16)
    grad_keyval = outer_sum(low_one, low_keyval)
    upstream_one = sum_one + against(low_keyval, key_value_weight)
    grad_gain_one = jnp.sum(upstream_one * normal_one, axis=(0, 1))
    grad_bias_one = jnp.sum(upstream_one, axis=(0, 1))
    grad_gain_two = jnp.sum(sum_two * normal_two, axis=(0, 1))
    grad_bias_two = jnp.sum(sum_two, axis=(0, 1))
    grad_tokens = (
        upstream
        + norm_back(upstream_one, normal_one, inverse_one, norm_gain_one)
        + norm_back(sum_two, normal_two, inverse_two, norm_gain_two)
    )
    grad_query, grad_output, grad_upward, grad_downward = lax.psum(
        (grad_query, grad_output, grad_upward, grad_downward), "dp"
    )
    grad_keyval, grad_gain_one, grad_bias_one, grad_gain_two, grad_bias_two = lax.psum(
        (grad_keyval, grad_gain_one, grad_bias_one, grad_gain_two, grad_bias_two), ("dp", "tp")
    )
    return (
        block_out,
        grad_tokens.astype(jnp.bfloat16),
        grad_query,
        grad_keyval,
        grad_output,
        grad_upward,
        grad_downward,
        grad_gain_one,
        grad_bias_one,
        grad_gain_two,
        grad_bias_two,
    )


def solution(mesh):
    in_specs = (
        P("dp", "tp", None),
        P("dp", "tp", None),
        P("dp"),
        P(),
        P(None, "tp"),
        P(),
        P("tp", None),
        P(None, "tp"),
        P("tp", None),
        P(),
        P(),
        P(),
        P(),
    )
    out_specs = (
        P("dp", "tp", None),
        P("dp", "tp", None),
        P(None, "tp"),
        P(),
        P("tp", None),
        P(None, "tp"),
        P("tp", None),
        P(),
        P(),
        P(),
        P(),
    )
    return jax.shard_map(shards, mesh=mesh, in_specs=in_specs, out_specs=out_specs, check_vma=False)
```

profile of v0, /device:TPU:0, one launch (start us, length us, event | category | flops | bytes accessed | tf_op | source)
XLA Modules:
  0.0 634.0 jit_solution(16872320583740692377)
XLA Ops:
  7.3 1.4 convert_reduce_fusion.1
  8.7 1.5 fusion.101
  10.2 2.9 fusion.89
  14.5 1.6 fusion.110
  16.9 0.8 iota_compare_fusion.5
  18.1 1.4 iota_compare_fusion.1
  20.2 0.9 broadcast_multiply_fusion
  21.1 23.4 %all-gather.4.cloned.1.call-done = bf16[1,2048,768]{2,1,0:T(8,128)(2,1)} async-done(((bf16[1,512,768]{2,1,0:T(8,128)(2,1)}), bf16[1,2048,768]{2,1,0:T(8,128)(2,1)}) %all-gather.4.cloned.1.call-update) | async-done | bytes 3145744 | tf_op jit(solution)/shard_map/all_gather | solution.py:87
  44.5 3.2 fusion.186
  48.2 2.1 fusion.58
  50.6 1.3 fusion.31
  51.9 2.1 fusion.25
  54.6 2.9 fusion.190
  57.5 2.0 fusion.187
  59.5 1.4 fusion.2
  60.9 2.2 copy-done.1
  63.1 2.8 fusion.189
  66.5 5.9 fusion.4
  72.3 6.7 %fusion = f32[512,3]{0,1:T(4,128)S(1)} fusion(f32[512,3,2048]{2,0,1:T(8,128)} %get-tuple-element.114, f32[512,3]{0,1:T(4,128)S(1)} %get-tuple-element.113, pred[512,2048]{1,0:T(8,128)(4,1)S(1)} %iota_compare_fusion), kind=kLoop, calls=%fused_computation.5 | loop fusion | flops 12581376 | bytes 13643776 | tf_op jit(solution)/shard_map/reduce_sum | solution.py:124
  79.1 7.8 %fusion.188 = (bf16[512,3,64]{0,2,1:T(8,128)(2,1)}, f32[512,3,64]{0,2,1:T(8,128)}) fusion(bf16[1,2048,128]{1,2,0:T(8,128)(2,1)S(1)} %get-tuple-element.107, f32[512,3,2048]{2,0,1:T(8,128)} %get-tuple-element.114, f32[512,3]{0,1:T(4,128)S(1)} %fusion, f32[512,3]{0,1:T(4,128)S(1)} %get-tuple-element.113, pred[512,2048]{1,0:T(8,128)(4,1)S(1)} %iota_compare_fusion), kind=kOutput, calls=%fused_computation.286 | convolution fusion | flops 418480128 | bytes 14499840 | tf_op jit(solution)/shard_map/sqhk,skd->sqhd/dot_general | solution.py:127
  88.2 1.6 copy-done.3
  91.0 3.2 fusion.61
  94.9 1.4 fusion.133
  96.4 0.8 multiply_convert_fusion.3
  97.2 1.1 copy-done.7
  99.0 1.9 fusion.116
  100.9 2.4 multiply_convert_fusion.2
  104.0 0.8 copy-done.6
  104.9 2.1 multiply_convert_fusion.1
  107.0 8.8 %multiply_convert_fusion = bf16[512,3,2048]{2,0,1:T(8,128)(2,1)S(1)} fusion(f32[512,3,2048]{2,0,1:T(8,128)} %get-tuple-element.114, f32[512,3]{0,1:T(4,128)S(1)} %get-tuple-element.80, f32[512,3]{0,1:T(4,128)S(1)} %copy-done.48, pred[512,2048]{1,0:T(8,128)(4,1)S(1)} %iota_compare_fusion, bf16[1,2048,128]{1,2,0:T(8,128)(2,1)S(1)} %copy-done.20, ...), kind=kOutput, calls=%fused_computation | convolution fusion | flops 421527552 | bytes 20398080 | tf_op jit(solution)/shard_map/sqhd,skd->sqhk/dot_general | solution.py:176
  116.1 0.9 fusion.76
  117.0 1.2 fusion.74
  118.5 1.6 fusion.67
  120.3 6.4 %fusion.70 = f32[1,2048,64]{1,2,0:T(8,128)S(1)} fusion(f32[512,3,2048]{2,0,1:T(8,128)} %get-tuple-element.114, f32[512,3]{0,1:T(4,128)S(1)} %copy-done.48, pred[512,2048]{1,0:T(8,128)(4,1)S(1)} %iota_compare_fusion, bf16[1,2048,3,64]{1,3,2,0:T(8,128)(2,1)S(1)} %bitcast.283), kind=kOutput, calls=%fused_computation.100 | convolution fusion | flops 415236096 | bytes 14360576 | tf_op jit(solution)/shard_map/sqhk,sqhd->skd/dot_general | solution.py:201
  127.8 0.8 pad_maximum_fusion.2
  128.7 17.5 %fusion.7 = (bf16[2048,768]{1,0:T(8,128)(2,1)}, f32[2048,768]{1,0:T(8,128)S(1)}) fusion(bf16[768,768]{1,0:T(8,128)(2,1)S(1)} %copy-done, bf16[1,2048,768]{2,1,0:T(8,128)(2,1)} %all-gather.6.cloned.1.call-done), kind=kOutput, calls=%fused_computation.19 | convolution fusion | flops 2518155264 | bytes 13762560 | tf_op jit(solution)/shard_map/dot_general | solution.py:138
  146.3 5.2 fusion.13
  151.5 1.7 copy-done.59
  153.2 4.0 fusion.54
  157.5 1.9 fusion.113
  159.5 3.1 fusion.112
  162.7 4.0 fusion.115
  166.7 2.0 fusion.114
  169.0 2.7 fusion.53
  171.8 4.9 fusion.191
  176.8 2.7 fusion.55
  179.8 3.6 fusion.34
  183.6 4.2 fusion.39
  187.8 4.2 fusion.32
  192.0 2.1 fusion.127
  194.2 3.6 fusion.47
  197.9 37.9 %reduce-scatter.7.cloned.1.call-done = bf16[1,512,768]{2,1,0:T(8,128)(2,1)} async-done(((bf16[1,2048,768]{2,1,0:T(8,128)(2,1)}), bf16[1,512,768]{2,1,0:T(8,128)(2,1)}) %reduce-scatter.7.cloned.1.call-update) | async-done | bytes 786448 | tf_op jit(solution)/shard_map/reduce_scatter | solution.py:221
  235.8 4.6 fusion.100
  240.4 40.1 %all-reduce.1 = (f32[768]{0:T(1024)}, f32[768]{0:T(1024)}, f32[768]{0:T(1024)}, f32[768]{0:T(1024)}) all-reduce(f32[768]{0:T(1024)} %get-tuple-element.67, f32[768]{0:T(1024)} %get-tuple-element.72, f32[768]{0:T(1024)} %get-tuple-element.74, f32[768]{0:T(1024)} %get-tuple-element.76), channel_id=1, replica_groups=mesh['dp'=8,'tp'=4] {'dp','tp'}, use_global_device_ids=true, to_apply=%region_29.30 | all-reduce | flops 3072 | bytes 24576 | tf_op jit(solution)/shard_map/psum | solution.py:246
  280.5 1.2 broadcast_multiply_fusion.1
  281.7 1.3 broadcast_multiply_fusion.3
  283.0 4.0 fusion.97
  287.0 122.9 %all-reduce.6.cloned.1.call-done = f32[768,128]{1,0:T(8,128)} async-done(((f32[768,128]{1,0:T(8,128)}), f32[768,128]{1,0:T(8,128)}) %all-reduce.6.cloned.1.call-update) | async-done | bytes 393232 | tf_op jit(solution)/shard_map/psum | solution.py:246
  410.0 206.7 %all-reduce.8.cloned.1.call-done = (f32[768,192]{0,1:T(8,128)}, f32[192,768]{1,0:T(8,128)}, f32[768,768]{1,0:T(8,128)}, f32[768,768]{1,0:T(8,128)}) async-done(((f32[768,192]{0,1:T(8,128)}, f32[192,768]{1,0:T(8,128)}, f32[768,768]{1,0:T(8,128)}, f32[768,768]{1,0:T(8,128)}), (f32[768,192]{0,1:T(8,128)}, f32[192,768]{1,0:T(8,128)}, f32[768,768]{1,0:T(8,128)}, ...) | async-done | bytes 5898256 | tf_op jit(solution)/shard_map/psum | solution.py:243
  616.7 2.1 copy.42
  618.7 1.8 copy.43
  620.5 1.9 copy.44
  622.4 3.2 copy.45
  625.6 1.4 copy.46
  (201 shorter events, 11.8 us)
Async XLA Ops:
  7.2 121.6 %copy-start = (bf16[768,768]{1,0:T(8,128)(2,1)S(1)}, bf16[768,768]{1,0:T(8,128)(2,1)}, u32[]{:S(2)}) copy-start(bf16[768,768]{1,0:T(8,128)(2,1)} %param.30) | copy-start | bytes 3538948
  7.2 6.6 %copy-start.57 = (f32[8]{0:T(128)S(1)}, f32[8]{0:T(128)}, u32[]{:S(2)}) copy-start(f32[8]{0:T(128)} %param.26) | copy-start | bytes 100
  7.2 7.3 %copy-start.12 = (bf16[1,512,768]{2,1,0:T(8,128)(2,1)S(1)}, bf16[1,512,768]{2,1,0:T(8,128)(2,1)}, u32[]{:S(2)}) copy-start(bf16[1,512,768]{2,1,0:T(8,128)(2,1)} %param.24) | copy-start | bytes 2359300
  7.2 37.3 %all-gather.4.cloned.1.call-start = ((), (), s32[]{:S(2)}) async-start(), calls=%async_computation.4 | async-start | bytes 3932160 | tf_op jit(solution)/shard_map/all_gather | solution.py:87
  8.7 9.4 %copy-start.38 = (f32[512]{0:T(512)}, f32[512]{0:T(512)S(1)}, u32[]{:S(2)}) copy-start(f32[512]{0:T(512)S(1)} %broadcast_multiply_fusion.5) | copy-start | bytes 6148
  10.2 34.3 %copy-start.32 = (bf16[768,128]{1,0:T(8,128)(2,1)S(1)}, bf16[768,128]{1,0:T(8,128)(2,1)}, u32[]{:S(2)}) copy-start(bf16[768,128]{1,0:T(8,128)(2,1)} %param.28) | copy-start | bytes 589828
  10.2 7.9 %copy-start.44 = (f32[512]{0:T(512)}, f32[512]{0:T(512)S(1)}, u32[]{:S(2)}) copy-start(f32[512]{0:T(512)S(1)} %add_rsqrt_fusion) | copy-start | bytes 6148
  13.1 77.8 %all-gather.8.cloned.1.call-start = ((), (), s32[]{:S(2)}) async-start(), calls=%async_computation.7 | async-start | bytes 3932160 | tf_op jit(solution)/shard_map/all_gather | solution.py:153
  16.1 112.6 %all-gather.6.cloned.1.call-start = ((), (), s32[]{:S(2)}) async-start(), calls=%async_computation.5 | async-start | bytes 3932160 | tf_op jit(solution)/shard_map/all_gather | solution.py:88
  16.8 175.2 %reduce-scatter.9.cloned.1.call-start = ((), (), s32[]{:S(2)}) async-start(), calls=%async_computation.9 | async-start | bytes 655360 | tf_op jit(solution)/shard_map/reduce_scatter | solution.py:227
  16.9 33.4 %copy-start.50 = (f32[8]{0:T(128)}, f32[8]{0:T(128)S(1)}, u32[]{:S(2)}) copy-start(f32[8]{0:T(128)S(1)} %multiply_power_fusion) | copy-start | bytes 100
  21.1 29.3 %copy-start.21 = (f32[2048,8]{0,1:T(8,128)}, f32[2048,8]{0,1:T(8,128)S(1)}, u32[]{:S(2)}) copy-start(f32[2048,8]{0,1:T(8,128)S(1)} %get-tuple-element.104) | copy-start | bytes 196612
  44.5 3.6 copy-start.8
  47.7 31.4 %copy-start.19 = (bf16[1,2048,128]{1,2,0:T(8,128)(2,1)}, bf16[1,2048,128]{1,2,0:T(8,128)(2,1)S(1)}, u32[]{:S(2)}) copy-start(bf16[1,2048,128]{1,2,0:T(8,128)(2,1)S(1)} %get-tuple-element.107) | copy-start | bytes 1572868
  47.8 18.7 %copy-start.15 = (bf16[1,2048,1,48]{1,3,2,0:T(8,128)(2,1)}, bf16[1,2048,1,48]{1,3,2,0:T(8,128)(2,1)S(1)}, u32[]{:S(2)}) copy-start(bf16[1,2048,1,48]{1,3,2,0:T(8,128)(2,1)S(1)} %slice.370) | copy-start | bytes 589828
  48.1 18.3 %copy-start.26 = (bf16[1,2048,1,8]{1,3,2,0:T(8,128)(2,1)}, bf16[1,2048,1,8]{1,3,2,0:T(8,128)(2,1)S(1)}, u32[]{:S(2)}) copy-start(bf16[1,2048,1,8]{1,3,2,0:T(8,128)(2,1)S(1)} %get-tuple-element.100) | copy-start | bytes 98308
  48.1 18.3 %copy-start.28 = (bf16[1,2048,1,8]{1,3,2,0:T(8,128)(2,1)}, bf16[1,2048,1,8]{1,3,2,0:T(8,128)(2,1)S(1)}, u32[]{:S(2)}) copy-start(bf16[1,2048,1,8]{1,3,2,0:T(8,128)(2,1)S(1)} %get-tuple-element.101) | copy-start | bytes 98308
  50.5 37.0 %copy-start.17 = (bf16[1,2048,64]{1,2,0:T(8,128)(2,1)}, bf16[1,2048,64]{1,2,0:T(8,128)(2,1)S(1)}, u32[]{:S(2)}) copy-start(bf16[1,2048,64]{1,2,0:T(8,128)(2,1)S(1)} %fusion.184) | copy-start | bytes 786436
  51.9 5.6 copy-start.11
  59.5 3.6 copy-start.1
  79.1 8.4 %copy-start.31 = (pred[512,512]{0,1:T(8,128)(4,1)S(1)}, pred[512,512]{0,1:T(8,128)(4,1)}, u32[]{:S(2)}) copy-start(pred[512,512]{0,1:T(8,128)(4,1)} %iota_compare_fusion.5) | copy-start | bytes 786436
  90.9 3.9 copy-start.20
  90.9 3.9 copy-start.41
  91.0 3.9 copy-start.43
  91.0 3.9 copy-start.61
  91.0 3.9 copy-start.62
  91.0 3.9 copy-start.63
  94.2 4.7 slice-start.5
  94.9 4.0 slice-start.6
  99.0 5.9 slice-start
  100.8 4.0 slice-start.1
  100.9 4.0 slice-start.2
  107.0 9.0 %copy-start.2 = (bf16[512,3,1536]{2,0,1:T(8,128)(2,1)}, bf16[512,3,1536]{2,0,1:T(8,128)(2,1)S(1)}, u32[]{:S(2)}) copy-start(bf16[512,3,1536]{2,0,1:T(8,128)(2,1)S(1)} %multiply_convert_fusion.1) | copy-start | bytes 14155780
  128.6 17.7 %copy-start.55 = (bf16[768,768]{1,0:T(8,128)(2,1)S(1)}, bf16[768,768]{1,0:T(8,128)(2,1)}, u32[]{:S(2)}) copy-start(bf16[768,768]{1,0:T(8,128)(2,1)} %param.31) | copy-start | bytes 3538948
  128.7 69.2 %reduce-scatter.11.cloned.1.call-start = ((), (), s32[]{:S(2)}) async-start(), calls=%async_computation.10 | async-start | bytes 3932160 | tf_op jit(solution)/shard_map/reduce_scatter | solution.py:224
  128.7 17.6 %copy-start.52 = (bf16[1,2048,768]{2,1,0:T(8,128)(2,1)S(1)}, bf16[1,2048,768]{2,1,0:T(8,128)(2,1)}, u32[]{:S(2)}) copy-start(bf16[1,2048,768]{2,1,0:T(8,128)(2,1)} %all-gather.8.cloned.1.call-done) | copy-start | bytes 9437188
  153.2 4.3 copy-start.18
  157.2 9.4 %slice-start.3 = ((s8[6291456]{0:T(1024)(128)(4,1)}), s8[2097152]{0:T(1024)(128)(4,1)S(1)}, s32[]{:S(2)}) async-start(s8[6291456]{0:T(1024)(128)(4,1)} %bitcast.269), calls=%async_computation.16 | async-start | bytes 4194304
  157.3 78.5 %reduce-scatter.7.cloned.1.call-start = ((), (), s32[]{:S(2)}) async-start(), calls=%async_computation.8 | async-start | bytes 3932160 | tf_op jit(solution)/shard_map/reduce_scatter | solution.py:221
  159.5 7.2 %slice-start.4 = ((s8[6291456]{0:T(1024)(128)(4,1)}), s8[4194304]{0:T(1024)(128)(4,1)S(1)}, s32[]{:S(2)}) async-start(s8[6291456]{0:T(1024)(128)(4,1)} %bitcast.269), calls=%async_computation.17 | async-start | bytes 8388608
  159.5 7.2 %copy-start.16 = (bf16[1,2048,1,48]{1,3,2,0:T(8,128)(2,1)S(1)}, bf16[1,2048,1,48]{1,3,2,0:T(8,128)(2,1)}, u32[]{:S(2)}) copy-start(bf16[1,2048,1,48]{1,3,2,0:T(8,128)(2,1)} %copy-done.15) | copy-start | bytes 589828
  159.5 7.2 %copy-start.27 = (bf16[1,2048,1,8]{1,3,2,0:T(8,128)(2,1)S(1)}, bf16[1,2048,1,8]{1,3,2,0:T(8,128)(2,1)}, u32[]{:S(2)}) copy-start(bf16[1,2048,1,8]{1,3,2,0:T(8,128)(2,1)} %copy-done.26) | copy-start | bytes 98308
  159.5 7.2 %copy-start.29 = (bf16[1,2048,1,8]{1,3,2,0:T(8,128)(2,1)S(1)}, bf16[1,2048,1,8]{1,3,2,0:T(8,128)(2,1)}, u32[]{:S(2)}) copy-start(bf16[1,2048,1,8]{1,3,2,0:T(8,128)(2,1)} %copy-done.28) | copy-start | bytes 98308
  171.7 111.3 %reduce-scatter.5.cloned.1.call-start = ((), (), s32[]{:S(2)}) async-start(), calls=%async_computation.6 | async-start | bytes 3932160 | tf_op jit(solution)/shard_map/reduce_scatter | solution.py:141
  171.8 5.0 copy-start.30
  171.8 5.0 copy-start.33
  171.8 5.0 copy-start.34
  171.8 5.0 copy-start.35
  171.8 5.0 copy-start.36
  179.5 230.5 %all-reduce.6.cloned.1.call-start = ((), (), s32[]{:S(2)}) async-start(), calls=%async_computation.11 | async-start | bytes 786432 | tf_op jit(solution)/shard_map/psum | solution.py:246
  179.8 3.7 copy-start.54
  179.8 3.8 copy-start.60
  183.6 4.2 copy-start.53
  183.6 4.2 copy-start.58
  187.8 4.2 copy-start.10
  194.1 41.7 %copy-start.9 = (bf16[1,512,768]{2,1,0:T(8,128)(2,1)S(1)}, bf16[1,512,768]{2,1,0:T(8,128)(2,1)}, u32[]{:S(2)}) copy-start(bf16[1,512,768]{2,1,0:T(8,128)(2,1)} %param.23) | copy-start | bytes 2359300
  194.1 41.7 %copy-start.39 = (f32[512]{0:T(512)S(1)}, f32[512]{0:T(512)}, u32[]{:S(2)}) copy-start(f32[512]{0:T(512)} %copy-done.38) | copy-start | bytes 6148
  194.1 41.7 %copy-start.45 = (f32[512]{0:T(512)S(1)}, f32[512]{0:T(512)}, u32[]{:S(2)}) copy-start(f32[512]{0:T(512)} %copy-done.44) | copy-start | bytes 6148
  194.1 41.7 %copy-start.46 = (f32[768]{0:T(1024)S(1)}, f32[768]{0:T(1024)}, u32[]{:S(2)}) copy-start(f32[768]{0:T(1024)} %param.32) | copy-start | bytes 9220
  194.1 41.7 %copy-start.47 = (f32[768]{0:T(1024)S(1)}, f32[768]{0:T(1024)}, u32[]{:S(2)}) copy-start(f32[768]{0:T(1024)} %param.34) | copy-start | bytes 9220
  194.1 422.5 %all-reduce.8.cloned.1.call-start = ((), (), s32[]{:S(2)}) async-start(), calls=%async_computation.12 | async-start | bytes 11796480 | tf_op jit(solution)/shard_map/psum | solution.py:243
  197.8 85.2 %copy-start.13 = (bf16[1,512,768]{2,1,0:T(8,128)(2,1)S(1)}, bf16[1,512,768]{2,1,0:T(8,128)(2,1)}, u32[]{:S(2)}) copy-start(bf16[1,512,768]{2,1,0:T(8,128)(2,1)} %param.24) | copy-start | bytes 2359300
  197.9 85.2 %copy-start.24 = (bf16[1,512,768]{2,1,0:T(8,128)(2,1)S(1)}, bf16[1,512,768]{2,1,0:T(8,128)(2,1)}, u32[]{:S(2)}) copy-start(bf16[1,512,768]{2,1,0:T(8,128)(2,1)} %reduce-scatter.11.cloned.1.call-done) | copy-start | bytes 2359300
  616.7 9.0 %copy-start.14 = (f32[768,768]{1,0:T(8,128)S(1)}, f32[768,768]{1,0:T(8,128)}, u32[]{:S(2)}) copy-start(f32[768,768]{1,0:T(8,128)} %get-tuple-element.140) | copy-start | bytes 7077892
  (16 other events, 31.0 us)
Sparse Core Ops, SparseCore 0:
  13.2 31.2 all-gather.3
  46.6 28.5 all-gather.7
  77.4 28.5 all-gather.5
  128.8 21.6 reduce-scatter.8
  157.4 37.9 reduce-scatter.10
  197.8 37.9 reduce-scatter.6
  238.5 38.1 reduce-scatter.4
  282.6 127.3 all-reduce.5
  415.1 201.4 all-reduce.7
where the time goes:
time: 640 us; the launch traced here: 634 us
  waiting for transfers between devices  392 us (61%)
  matrix products  132 us (21%)
  blocking collectives  40.1 us (6%)
  other arithmetic  33.5 us (5%)
  local copies, waits for them, and re-layouts  19.8 us (3%)
  between operations  16.1 us (3%)
    psum x1, waiting for transfers between devices, shards(): lax.psum((grad_query, grad_output, grad_upward, grad_downward), 'dp')  207 us
    psum x1, waiting for transfers between devices, shards(): lax.psum((grad_keyval, grad_gain_one, grad_bias_one, grad_gain_two, grad_...  123 us
    psum x1, blocking collectives, shards(): lax.psum((grad_keyval, grad_gain_one, grad_bias_one, grad_gain_two, grad_...  40.1 us
    reduce_scatter x1, waiting for transfers between devices, shards(): lax.psum_scatter(norm_part_one.astype(jnp.bfloat16), 'tp', scatter_dimens...  37.9 us
    all_gather x1, waiting for transfers between devices, shards(): lax.all_gather(low_one, 'tp', axis=1, tiled=True)  23.4 us
    dot_general x5, matrix products, against(): lax.dot_general(left, weight, (((2,), (1,)), ((), ())), preferred_element...  19.8 us
    unnamed x147, local copies, waits for them, and re-layouts  19.6 us
    dot_general x5, matrix products, outer_sum(): lax.dot_general(left, right, (((0, 1), (0, 1)), ((), ())), preferred_elem...  17.6 us
  transfers between devices with their start and end apart: 9, of which 4 were waited for; matrix products, arithmetic and copies ran while one was open for 25% of the time, Pallas kernels for 0%

commit v1 on v0

--- a/solution.py
+++ b/solution.py
@@ -5,6 +5,12 @@
 
 HD = 64
 ROT = 16
+
+
+def plan_sums_all(u):
+    for ii in ("tp", "dp"):
+        u = lax.psum(u, ii)
+    return u
 
 
 def layer_norm(values, gain_vec, shift_vec):
@@ -243,8 +249,8 @@
     grad_query, grad_output, grad_upward, grad_downward = lax.psum(
         (grad_query, grad_output, grad_upward, grad_downward), "dp"
     )
-    grad_keyval, grad_gain_one, grad_bias_one, grad_gain_two, grad_bias_two = lax.psum(
-        (grad_keyval, grad_gain_one, grad_bias_one, grad_gain_two, grad_bias_two), ("dp", "tp")
+    grad_keyval, grad_gain_one, grad_bias_one, grad_gain_two, grad_bias_two = plan_sums_all(
+        (grad_keyval, grad_gain_one, grad_bias_one, grad_gain_two, grad_bias_two)
     )
     return (
         block_out,

time: 640 us -> 553 us (0.86)
  waiting for transfers between devices: 392 us -> 295 us
  blocking collectives: 40.1 us -> 49.2 us
    psum x1, waiting for transfers between devices: 123 us -> 0.02 us  [plan_sums_all(): u = lax.psum(u, ii)]
    reduce_scatter x1, waiting for transfers between devices: 0.02 us -> 28.8 us  [shards(): lax.psum_scatter(norm_part_two.astype(jnp.bfloat16), 'tp', scatter_dimens...]
    psum x1 -> x2, blocking collectives: 40.1 us -> 49.2 us  [plan_sums_all(): u = lax.psum(u, ii)]
    unnamed x147 -> x145, local copies, waits for them, and re-layouts: 19.6 us -> 17.7 us
  transfers between devices with their start and end apart: 9 -> 9, of which waited for: 4 -> 4; matrix products, arithmetic and copies ran while one was open for 25% -> 29% of each run, Pallas kernels for 0% -> 0%
where the time goes in v1:
time: 553 us; the launch traced here: 548 us
  waiting for transfers between devices  295 us (53%)
  matrix products  135 us (24%)
  blocking collectives  49.2 us (9%)
  other arithmetic  33.5 us (6%)
  local copies, waits for them, and re-layouts  17.9 us (3%)
  between operations  16 us (3%)
    psum x1, waiting for transfers between devices, shards(): lax.psum((grad_query, grad_output, grad_upward, grad_downward), 'dp')  202 us
    psum x2, blocking collectives, plan_sums_all(): u = lax.psum(u, ii)  49.2 us
    reduce_scatter x1, waiting for transfers between devices, shards(): lax.psum_scatter(norm_part_one.astype(jnp.bfloat16), 'tp', scatter_dimens...  40.6 us
    reduce_scatter x1, waiting for transfers between devices, shards(): lax.psum_scatter(norm_part_two.astype(jnp.bfloat16), 'tp', scatter_dimens...  28.8 us
    all_gather x1, waiting for transfers between devices, shards(): lax.all_gather(low_one, 'tp', axis=1, tiled=True)  23.4 us
    dot_general x5, matrix products, against(): lax.dot_general(left, weight, (((2,), (1,)), ((), ())), preferred_element...  23 us
    unnamed x145, local copies, waits for them, and re-layouts  17.7 us
    dot_general x1, matrix products, shards(): jnp.dot(rows_two, up_weight, preferred_element_type=jnp.float32)  17.5 us
  transfers between devices with their start and end apart: 9, of which 4 were waited for; matrix products, arithmetic and copies ran while one was open for 29% of the time, Pallas kernels for 0%

profile of v1, /device:TPU:0, one launch (start us, length us, event | category | flops | bytes accessed | tf_op | source)
XLA Modules:
  0.0 547.7 jit_solution(8053667522698123851)
XLA Ops:
  7.3 1.4 convert_reduce_fusion.1
  8.7 1.5 fusion.101
  10.2 2.9 fusion.89
  14.4 1.6 fusion.110
  16.9 0.8 iota_compare_fusion.5
  18.1 1.4 iota_compare_fusion.1
  20.1 0.9 broadcast_multiply_fusion
  21.1 23.4 %all-gather.4.cloned.1.call-done = bf16[1,2048,768]{2,1,0:T(8,128)(2,1)} async-done(((bf16[1,512,768]{2,1,0:T(8,128)(2,1)}), bf16[1,2048,768]{2,1,0:T(8,128)(2,1)}) %all-gather.4.cloned.1.call-update) | async-done | bytes 3145744 | tf_op jit(solution)/shard_map/all_gather | solution.py:93
  44.5 3.2 fusion.186
  48.2 2.1 fusion.58
  50.6 1.3 fusion.31
  51.9 2.1 fusion.25
  54.6 2.9 fusion.190
  57.5 2.0 fusion.187
  59.5 1.4 fusion.2
  60.9 2.2 copy-done.1
  63.1 2.8 fusion.189
  66.5 5.9 %fusion.4 = (f32[512,3]{0,1:T(4,128)S(1)}, f32[512,3,2048]{2,0,1:T(8,128)}) fusion(pred[512,2048]{1,0:T(8,128)(4,1)S(1)} %iota_compare_fusion, bf16[1,2048,1,48]{1,3,2,0:T(8,128)(2,1)S(1)} %slice.370, bf16[1,2048,1,8]{1,3,2,0:T(8,128)(2,1)S(1)} %get-tuple-element.106, bf16[1,2048,1,8]{1,3,2,0:T(8,128)(2,1)S(1)} %get-tuple-element.105, ...), kind=kOutput, calls=%fused_computation.16 | convolution fusion | flops 412875264 | bytes 14096384 | tf_op jit(solution)/shard_map/sqhd,skd->sqhk/dot_general | solution.py:111
  72.3 6.7 %fusion = f32[512,3]{0,1:T(4,128)S(1)} fusion(f32[512,3,2048]{2,0,1:T(8,128)} %get-tuple-element.119, f32[512,3]{0,1:T(4,128)S(1)} %get-tuple-element.118, pred[512,2048]{1,0:T(8,128)(4,1)S(1)} %iota_compare_fusion), kind=kLoop, calls=%fused_computation.5 | loop fusion | flops 12581376 | bytes 13643776 | tf_op jit(solution)/shard_map/reduce_sum | solution.py:130
  79.1 7.8 %fusion.188 = (bf16[512,3,64]{0,2,1:T(8,128)(2,1)}, f32[512,3,64]{0,2,1:T(8,128)}) fusion(bf16[1,2048,128]{1,2,0:T(8,128)(2,1)S(1)} %get-tuple-element.112, f32[512,3,2048]{2,0,1:T(8,128)} %get-tuple-element.119, f32[512,3]{0,1:T(4,128)S(1)} %fusion, f32[512,3]{0,1:T(4,128)S(1)} %get-tuple-element.118, pred[512,2048]{1,0:T(8,128)(4,1)S(1)} %iota_compare_fusion), kind=kOutput, calls=%fused_computation.286 | convolution fusion | flops 418480128 | bytes 14499840 | tf_op jit(solution)/shard_map/sqhk,skd->sqhd/dot_general | solution.py:133
  88.3 1.6 copy-done.3
  91.0 3.2 fusion.61
  95.0 1.4 fusion.133
  96.4 0.8 multiply_convert_fusion.3
  97.3 1.1 copy-done.7
  99.0 1.9 fusion.116
  100.9 2.4 multiply_convert_fusion.2
  104.1 0.8 copy-done.6
  104.9 2.1 multiply_convert_fusion.1
  107.1 8.8 %multiply_convert_fusion = bf16[512,3,2048]{2,0,1:T(8,128)(2,1)S(1)} fusion(f32[512,3,2048]{2,0,1:T(8,128)} %get-tuple-element.119, f32[512,3]{0,1:T(4,128)S(1)} %get-tuple-element.80, f32[512,3]{0,1:T(4,128)S(1)} %copy-done.48, pred[512,2048]{1,0:T(8,128)(4,1)S(1)} %iota_compare_fusion, bf16[1,2048,128]{1,2,0:T(8,128)(2,1)S(1)} %copy-done.20, ...), kind=kOutput, calls=%fused_computation | convolution fusion | flops 421527552 | bytes 20398080 | tf_op jit(solution)/shard_map/sqhd,skd->sqhk/dot_general | solution.py:182
  116.1 0.9 fusion.76
  117.0 1.2 fusion.74
  118.5 1.6 fusion.67
  120.4 6.4 %fusion.70 = f32[1,2048,64]{1,2,0:T(8,128)S(1)} fusion(f32[512,3,2048]{2,0,1:T(8,128)} %get-tuple-element.119, f32[512,3]{0,1:T(4,128)S(1)} %copy-done.48, pred[512,2048]{1,0:T(8,128)(4,1)S(1)} %iota_compare_fusion, bf16[1,2048,3,64]{1,3,2,0:T(8,128)(2,1)S(1)} %bitcast.283), kind=kOutput, calls=%fused_computation.100 | convolution fusion | flops 415236096 | bytes 14360576 | tf_op jit(solution)/shard_map/sqhk,sqhd->skd/dot_general | solution.py:207
  127.8 0.8 pad_maximum_fusion.2
  128.8 17.5 %fusion.7 = (bf16[2048,768]{1,0:T(8,128)(2,1)}, f32[2048,768]{1,0:T(8,128)S(1)}) fusion(bf16[768,768]{1,0:T(8,128)(2,1)S(1)} %copy-done, bf16[1,2048,768]{2,1,0:T(8,128)(2,1)} %all-gather.6.cloned.1.call-done), kind=kOutput, calls=%fused_computation.19 | convolution fusion | flops 2518155264 | bytes 13762560 | tf_op jit(solution)/shard_map/dot_general | solution.py:144
  146.3 6.2 %fusion.13 = bf16[2048,768]{1,0:T(8,128)(2,1)} fusion(f32[2048,768]{1,0:T(8,128)S(1)} %get-tuple-element.123, bf16[768,768]{1,0:T(8,128)(2,1)S(1)} %copy-done.55, bf16[1,2048,768]{2,1,0:T(8,128)(2,1)S(1)} %copy-done.52), kind=kOutput, calls=%fused_computation.25 | convolution fusion | flops 2431647744 | bytes 13762560 | tf_op jit(solution)/shard_map/dot_general | solution.py:60
  152.5 2.1 fusion.127
  154.8 6.2 %fusion.54 = bf16[1,2048,768]{2,1,0:T(8,128)(2,1)} fusion(bf16[2048,768]{1,0:T(8,128)(2,1)} %fusion.13, bf16[768,768]{1,0:T(8,128)(2,1)S(1)} %copy-done), kind=kOutput, calls=%fused_computation.86 | convolution fusion | flops 2417491968 | bytes 7471104 | tf_op jit(solution)/shard_map/dot_general | solution.py:60
  161.2 1.9 fusion.113
  163.2 3.1 fusion.112
  166.3 3.9 fusion.115
  170.3 2.0 fusion.114
  172.5 2.7 fusion.53
  175.4 5.0 fusion.191
  180.4 2.7 fusion.55
  183.4 3.6 fusion.47
  187.0 3.5 fusion.34
  190.5 4.2 fusion.39
  194.7 4.2 fusion.32
  199.0 28.8 %reduce-scatter.11.cloned.1.call-done = bf16[1,512,768]{2,1,0:T(8,128)(2,1)} async-done(((bf16[1,2048,768]{2,1,0:T(8,128)(2,1)}), bf16[1,512,768]{2,1,0:T(8,128)(2,1)}) %reduce-scatter.11.cloned.1.call-update) | async-done | bytes 786448 | tf_op jit(solution)/shard_map/reduce_scatter | solution.py:230
  227.7 40.6 %reduce-scatter.7.cloned.1.call-done = bf16[1,512,768]{2,1,0:T(8,128)(2,1)} async-done(((bf16[1,2048,768]{2,1,0:T(8,128)(2,1)}), bf16[1,512,768]{2,1,0:T(8,128)(2,1)}) %reduce-scatter.7.cloned.1.call-update) | async-done | bytes 786448 | tf_op jit(solution)/shard_map/reduce_scatter | solution.py:227
  268.4 4.6 fusion.100
  273.0 11.3 %all-reduce.3 = (f32[768]{0:T(1024)}, f32[768]{0:T(1024)}, f32[768]{0:T(1024)}, f32[768]{0:T(1024)}) all-reduce(f32[768]{0:T(1024)} %get-tuple-element.67, f32[768]{0:T(1024)} %get-tuple-element.72, f32[768]{0:T(1024)} %get-tuple-element.74, f32[768]{0:T(1024)} %get-tuple-element.76), channel_id=1, replica_groups=mesh['dp'=8,'tp'=4] {'tp'}, use_global_device_ids=true, to_apply=%region_30.31 | all-reduce | flops 3072 | bytes 24576 | tf_op jit(solution)/shard_map/psum | solution.py:12
  284.4 37.8 %all-reduce.1 = (f32[768]{0:T(1024)}, f32[768]{0:T(1024)}, f32[768]{0:T(1024)}, f32[768]{0:T(1024)}) all-reduce(f32[768]{0:T(1024)} %get-tuple-element.90, f32[768]{0:T(1024)} %get-tuple-element.91, f32[768]{0:T(1024)} %get-tuple-element.92, f32[768]{0:T(1024)} %get-tuple-element.93), channel_id=1, replica_groups=mesh['dp'=8,'tp'=4] {'dp'}, use_global_device_ids=true, to_apply=%region_31.32 | all-reduce | flops 3072 | bytes 24576 | tf_op jit(solution)/shard_map/psum | solution.py:12
  322.2 1.3 broadcast_multiply_fusion.1
  323.5 1.3 broadcast_multiply_fusion.3
  324.7 4.0 fusion.97
  328.7 201.6 %all-reduce.9.cloned.1.call-done = (f32[768,192]{0,1:T(8,128)}, f32[768,128]{1,0:T(8,128)}, f32[192,768]{1,0:T(8,128)}, f32[768,768]{1,0:T(8,128)}, f32[768,768]{1,0:T(8,128)}) async-done(((f32[768,192]{0,1:T(8,128)}, f32[768,128]{1,0:T(8,128)}, f32[192,768]{1,0:T(8,128)}, f32[768,768]{1,0:T(8,128)}, f32[768,768]{1,0:T(8,128)}), (f32[768,192]{0,1:T(8,128)}, f32[768,128]{1,0:T(8,128)}, f32[192,768]{1,0:T(8,128)}, ...) | async-done | bytes 6291472 | tf_op jit(solution)/shard_map/psum | solution.py:249
  530.4 2.1 copy.43
  532.4 1.8 copy.44
  534.2 1.9 copy.45
  536.1 3.2 copy.46
  539.3 1.4 copy.47
  (200 shorter events, 11.6 us)
Async XLA Ops:
  7.2 121.6 %copy-start = (bf16[768,768]{1,0:T(8,128)(2,1)S(1)}, bf16[768,768]{1,0:T(8,128)(2,1)}, u32[]{:S(2)}) copy-start(bf16[768,768]{1,0:T(8,128)(2,1)} %param.30) | copy-start | bytes 3538948
  7.2 6.6 %copy-start.57 = (f32[8]{0:T(128)S(1)}, f32[8]{0:T(128)}, u32[]{:S(2)}) copy-start(f32[8]{0:T(128)} %param.26) | copy-start | bytes 100
  7.2 7.2 %copy-start.12 = (bf16[1,512,768]{2,1,0:T(8,128)(2,1)S(1)}, bf16[1,512,768]{2,1,0:T(8,128)(2,1)}, u32[]{:S(2)}) copy-start(bf16[1,512,768]{2,1,0:T(8,128)(2,1)} %param.24) | copy-start | bytes 2359300
  7.2 37.3 %all-gather.4.cloned.1.call-start = ((), (), s32[]{:S(2)}) async-start(), calls=%async_computation.4 | async-start | bytes 3932160 | tf_op jit(solution)/shard_map/all_gather | solution.py:93
  8.7 9.4 %copy-start.38 = (f32[512]{0:T(512)}, f32[512]{0:T(512)S(1)}, u32[]{:S(2)}) copy-start(f32[512]{0:T(512)S(1)} %broadcast_multiply_fusion.5) | copy-start | bytes 6148
  10.2 34.3 %copy-start.32 = (bf16[768,128]{1,0:T(8,128)(2,1)S(1)}, bf16[768,128]{1,0:T(8,128)(2,1)}, u32[]{:S(2)}) copy-start(bf16[768,128]{1,0:T(8,128)(2,1)} %param.28) | copy-start | bytes 589828
  10.2 7.8 %copy-start.44 = (f32[512]{0:T(512)}, f32[512]{0:T(512)S(1)}, u32[]{:S(2)}) copy-start(f32[512]{0:T(512)S(1)} %add_rsqrt_fusion) | copy-start | bytes 6148
  13.1 77.8 %all-gather.8.cloned.1.call-start = ((), (), s32[]{:S(2)}) async-start(), calls=%async_computation.7 | async-start | bytes 3932160 | tf_op jit(solution)/shard_map/all_gather | solution.py:159
  16.1 112.7 %all-gather.6.cloned.1.call-start = ((), (), s32[]{:S(2)}) async-start(), calls=%async_computation.5 | async-start | bytes 3932160 | tf_op jit(solution)/shard_map/all_gather | solution.py:94
  16.8 135.7 %reduce-scatter.9.cloned.1.call-start = ((), (), s32[]{:S(2)}) async-start(), calls=%async_computation.9 | async-start | bytes 655360 | tf_op jit(solution)/shard_map/reduce_scatter | solution.py:233
  16.9 33.4 %copy-start.50 = (f32[8]{0:T(128)}, f32[8]{0:T(128)S(1)}, u32[]{:S(2)}) copy-start(f32[8]{0:T(128)S(1)} %multiply_power_fusion) | copy-start | bytes 100
  21.1 29.3 %copy-start.21 = (f32[2048,8]{0,1:T(8,128)}, f32[2048,8]{0,1:T(8,128)S(1)}, u32[]{:S(2)}) copy-start(f32[2048,8]{0,1:T(8,128)S(1)} %get-tuple-element.109) | copy-start | bytes 196612
  44.5 3.6 copy-start.8
  47.7 31.4 %copy-start.19 = (bf16[1,2048,128]{1,2,0:T(8,128)(2,1)}, bf16[1,2048,128]{1,2,0:T(8,128)(2,1)S(1)}, u32[]{:S(2)}) copy-start(bf16[1,2048,128]{1,2,0:T(8,128)(2,1)S(1)} %get-tuple-element.112) | copy-start | bytes 1572868
  47.8 18.7 %copy-start.15 = (bf16[1,2048,1,48]{1,3,2,0:T(8,128)(2,1)}, bf16[1,2048,1,48]{1,3,2,0:T(8,128)(2,1)S(1)}, u32[]{:S(2)}) copy-start(bf16[1,2048,1,48]{1,3,2,0:T(8,128)(2,1)S(1)} %slice.370) | copy-start | bytes 589828
  48.1 18.3 %copy-start.26 = (bf16[1,2048,1,8]{1,3,2,0:T(8,128)(2,1)}, bf16[1,2048,1,8]{1,3,2,0:T(8,128)(2,1)S(1)}, u32[]{:S(2)}) copy-start(bf16[1,2048,1,8]{1,3,2,0:T(8,128)(2,1)S(1)} %get-tuple-element.105) | copy-start | bytes 98308
  48.1 18.3 %copy-start.28 = (bf16[1,2048,1,8]{1,3,2,0:T(8,128)(2,1)}, bf16[1,2048,1,8]{1,3,2,0:T(8,128)(2,1)S(1)}, u32[]{:S(2)}) copy-start(bf16[1,2048,1,8]{1,3,2,0:T(8,128)(2,1)S(1)} %get-tuple-element.106) | copy-start | bytes 98308
  50.5 37.1 %copy-start.17 = (bf16[1,2048,64]{1,2,0:T(8,128)(2,1)}, bf16[1,2048,64]{1,2,0:T(8,128)(2,1)S(1)}, u32[]{:S(2)}) copy-start(bf16[1,2048,64]{1,2,0:T(8,128)(2,1)S(1)} %fusion.184) | copy-start | bytes 786436
  51.9 5.6 %copy-start.11 = (f32[512,3,1024]{2,0,1:T(8,128)}, f32[512,3,1024]{2,0,1:T(8,128)S(1)}, u32[]{:S(2)}) copy-start(f32[512,3,1024]{2,0,1:T(8,128)S(1)} %get-tuple-element.115) | copy-start | bytes 18874372
  59.5 3.6 copy-start.1
  79.1 8.5 %copy-start.31 = (pred[512,512]{0,1:T(8,128)(4,1)S(1)}, pred[512,512]{0,1:T(8,128)(4,1)}, u32[]{:S(2)}) copy-start(pred[512,512]{0,1:T(8,128)(4,1)} %iota_compare_fusion.5) | copy-start | bytes 786436
  91.0 3.9 copy-start.20
  91.0 3.9 copy-start.41
  91.0 3.9 copy-start.43
  91.0 3.9 copy-start.60
  91.0 3.9 copy-start.61
  91.0 3.9 copy-start.62
  94.3 4.7 slice-start.5
  95.0 4.0 slice-start.6
  99.0 5.9 %slice-start = ((s8[9437184]{0:T(1024)(128)(4,1)}), s8[4194304]{0:T(1024)(128)(4,1)S(1)}, s32[]{:S(2)}) async-start(s8[9437184]{0:T(1024)(128)(4,1)} %bitcast.267), calls=%async_computation.13 | async-start | bytes 8388608
  100.9 4.0 slice-start.1
  100.9 4.0 slice-start.2
  107.1 9.0 %copy-start.2 = (bf16[512,3,1536]{2,0,1:T(8,128)(2,1)}, bf16[512,3,1536]{2,0,1:T(8,128)(2,1)S(1)}, u32[]{:S(2)}) copy-start(bf16[512,3,1536]{2,0,1:T(8,128)(2,1)S(1)} %multiply_convert_fusion.1) | copy-start | bytes 14155780
  128.7 17.6 %copy-start.55 = (bf16[768,768]{1,0:T(8,128)(2,1)S(1)}, bf16[768,768]{1,0:T(8,128)(2,1)}, u32[]{:S(2)}) copy-start(bf16[768,768]{1,0:T(8,128)(2,1)} %param.31) | copy-start | bytes 3538948
  128.7 70.3 %all-reduce.7.cloned.1.call-start = ((), (), s32[]{:S(2)}) async-start(), calls=%async_computation.11 | async-start | bytes 786432 | tf_op jit(solution)/shard_map/psum | solution.py:12
  128.8 17.5 %copy-start.52 = (bf16[1,2048,768]{2,1,0:T(8,128)(2,1)S(1)}, bf16[1,2048,768]{2,1,0:T(8,128)(2,1)}, u32[]{:S(2)}) copy-start(bf16[1,2048,768]{2,1,0:T(8,128)(2,1)} %all-gather.8.cloned.1.call-done) | copy-start | bytes 9437188
  146.3 6.2 %copy-start.10 = (bf16[1,512,768]{2,1,0:T(8,128)(2,1)S(1)}, bf16[1,512,768]{2,1,0:T(8,128)(2,1)}, u32[]{:S(2)}) copy-start(bf16[1,512,768]{2,1,0:T(8,128)(2,1)} %get-tuple-element.99) | copy-start | bytes 2359300
  154.6 6.6 %copy-start.18 = (bf16[1,2048,64]{1,2,0:T(8,128)(2,1)S(1)}, bf16[1,2048,64]{1,2,0:T(8,128)(2,1)}, u32[]{:S(2)}) copy-start(bf16[1,2048,64]{1,2,0:T(8,128)(2,1)} %copy-done.17) | copy-start | bytes 786436
  154.6 73.2 %reduce-scatter.11.cloned.1.call-start = ((), (), s32[]{:S(2)}) async-start(), calls=%async_computation.10 | async-start | bytes 3932160 | tf_op jit(solution)/shard_map/reduce_scatter | solution.py:230
  161.1 9.1 %slice-start.3 = ((s8[6291456]{0:T(1024)(128)(4,1)}), s8[2097152]{0:T(1024)(128)(4,1)S(1)}, s32[]{:S(2)}) async-start(s8[6291456]{0:T(1024)(128)(4,1)} %bitcast.269), calls=%async_computation.16 | async-start | bytes 4194304
  161.1 107.3 %reduce-scatter.7.cloned.1.call-start = ((), (), s32[]{:S(2)}) async-start(), calls=%async_computation.8 | async-start | bytes 3932160 | tf_op jit(solution)/shard_map/reduce_scatter | solution.py:227
  163.1 7.1 %slice-start.4 = ((s8[6291456]{0:T(1024)(128)(4,1)}), s8[4194304]{0:T(1024)(128)(4,1)S(1)}, s32[]{:S(2)}) async-start(s8[6291456]{0:T(1024)(128)(4,1)} %bitcast.269), calls=%async_computation.17 | async-start | bytes 8388608
  163.1 7.1 %copy-start.16 = (bf16[1,2048,1,48]{1,3,2,0:T(8,128)(2,1)S(1)}, bf16[1,2048,1,48]{1,3,2,0:T(8,128)(2,1)}, u32[]{:S(2)}) copy-start(bf16[1,2048,1,48]{1,3,2,0:T(8,128)(2,1)} %copy-done.15) | copy-start | bytes 589828
  163.1 7.1 %copy-start.27 = (bf16[1,2048,1,8]{1,3,2,0:T(8,128)(2,1)S(1)}, bf16[1,2048,1,8]{1,3,2,0:T(8,128)(2,1)}, u32[]{:S(2)}) copy-start(bf16[1,2048,1,8]{1,3,2,0:T(8,128)(2,1)} %copy-done.26) | copy-start | bytes 98308
  163.1 7.1 %copy-start.29 = (bf16[1,2048,1,8]{1,3,2,0:T(8,128)(2,1)S(1)}, bf16[1,2048,1,8]{1,3,2,0:T(8,128)(2,1)}, u32[]{:S(2)}) copy-start(bf16[1,2048,1,8]{1,3,2,0:T(8,128)(2,1)} %copy-done.28) | copy-start | bytes 98308
  175.2 149.5 %reduce-scatter.5.cloned.1.call-start = ((), (), s32[]{:S(2)}) async-start(), calls=%async_computation.6 | async-start | bytes 3932160 | tf_op jit(solution)/shard_map/reduce_scatter | solution.py:147
  175.3 5.0 copy-start.30
  175.3 5.0 copy-start.33
  175.3 5.0 copy-start.34
  175.3 5.0 copy-start.35
  175.3 5.0 copy-start.36
  183.1 347.3 %all-reduce.9.cloned.1.call-start = ((), (), s32[]{:S(2)}) async-start(), calls=%async_computation.12 | async-start | bytes 12582912 | tf_op jit(solution)/shard_map/psum | solution.py:249
  183.4 7.1 %copy-start.54 = (bf16[1,2048,768]{2,1,0:T(8,128)(2,1)S(1)}, bf16[1,2048,768]{2,1,0:T(8,128)(2,1)}, u32[]{:S(2)}) copy-start(bf16[1,2048,768]{2,1,0:T(8,128)(2,1)} %all-gather.6.cloned.1.call-done) | copy-start | bytes 9437188
  183.4 7.1 %copy-start.59 = (bf16[2048,768]{1,0:T(8,128)(2,1)S(1)}, bf16[2048,768]{1,0:T(8,128)(2,1)}, u32[]{:S(2)}) copy-start(bf16[2048,768]{1,0:T(8,128)(2,1)} %fusion.13) | copy-start | bytes 9437188
  190.5 4.2 copy-start.53
  190.5 4.2 copy-start.58
  198.9 69.5 %copy-start.9 = (bf16[1,512,768]{2,1,0:T(8,128)(2,1)S(1)}, bf16[1,512,768]{2,1,0:T(8,128)(2,1)}, u32[]{:S(2)}) copy-start(bf16[1,512,768]{2,1,0:T(8,128)(2,1)} %param.23) | copy-start | bytes 2359300
  198.9 69.5 %copy-start.39 = (f32[512]{0:T(512)S(1)}, f32[512]{0:T(512)}, u32[]{:S(2)}) copy-start(f32[512]{0:T(512)} %copy-done.38) | copy-start | bytes 6148
  198.9 69.5 %copy-start.45 = (f32[512]{0:T(512)S(1)}, f32[512]{0:T(512)}, u32[]{:S(2)}) copy-start(f32[512]{0:T(512)} %copy-done.44) | copy-start | bytes 6148
  198.9 69.5 %copy-start.46 = (f32[768]{0:T(1024)S(1)}, f32[768]{0:T(1024)}, u32[]{:S(2)}) copy-start(f32[768]{0:T(1024)} %param.32) | copy-start | bytes 9220
  198.9 69.5 %copy-start.47 = (f32[768]{0:T(1024)S(1)}, f32[768]{0:T(1024)}, u32[]{:S(2)}) copy-start(f32[768]{0:T(1024)} %param.34) | copy-start | bytes 9220
  199.0 125.8 %copy-start.13 = (bf16[1,512,768]{2,1,0:T(8,128)(2,1)S(1)}, bf16[1,512,768]{2,1,0:T(8,128)(2,1)}, u32[]{:S(2)}) copy-start(bf16[1,512,768]{2,1,0:T(8,128)(2,1)} %param.24) | copy-start | bytes 2359300
  227.7 97.0 %copy-start.24 = (bf16[1,512,768]{2,1,0:T(8,128)(2,1)S(1)}, bf16[1,512,768]{2,1,0:T(8,128)(2,1)}, u32[]{:S(2)}) copy-start(bf16[1,512,768]{2,1,0:T(8,128)(2,1)} %reduce-scatter.11.cloned.1.call-done) | copy-start | bytes 2359300
  530.4 9.0 %copy-start.14 = (f32[768,768]{1,0:T(8,128)S(1)}, f32[768,768]{1,0:T(8,128)}, u32[]{:S(2)}) copy-start(f32[768,768]{1,0:T(8,128)} %get-tuple-element.145) | copy-start | bytes 7077892
  (15 other events, 29.2 us)
Sparse Core Ops, SparseCore 0:
  13.2 31.2 all-gather.3
  46.6 28.5 all-gather.7
  77.4 28.5 all-gather.5
  128.8 21.6 reduce-scatter.8
  154.7 32.6 all-reduce.6
  189.8 37.9 reduce-scatter.10
  230.4 37.9 reduce-scatter.6
  270.9 37.9 reduce-scatter.4
  315.1 215.2 all-reduce.8
